TPU v7x, 768 devices: a whole 4x8x12 slice. The times are simulated.
768 devices in a mesh: row: 32 (over y, x), col: 24 (over z, core).
Axes of the slice: x: 4, y: 8, z: 12, core: 2. Of those that a mesh axis runs over, the one named last changes fastest.
Arguments:
- covariance: float32 [3, 32, 4, 24, 128, 128], P(None, 'row', None, 'col'), may hold values from -2 to 2, as said below
- tile_mask: int32 [96, 96], replicated, may hold values from 0 to 1, as said below
Outputs:
- updated: bfloat16 [3, 32, 4, 24, 128, 128], P(None, 'row', None, 'col')
Inputs may be any that keep to these rules, and one draw needn't show every extreme that they name: `covariance`: symmetric; the masked leading block of order 512 is positive definite. `tile_mask`: symmetric; tiles on the diagonal and next to it, and tiles whose row and column both lie among the first 4 tile rows, are all ones.
All inputs are finite; a program needn't handle non-finite values.
Results may differ from a plain program's by a relative error of at most 0.001.
Values sent between devices are 32-bit elements; how exact they have to be, the bound alone decides.
A program may use at most 32 MiB of HBM per device.

v0:
```python
import jax
import jax.numpy as jnp
from jax import lax
from jax.sharding import PartitionSpec as P

TPP = 2
PANELS = 2


def spread(value, axis, source):
    kept = jnp.where(lax.axis_index(axis) == source, value, 0).astype(value.dtype)
    return lax.psum(kept, axis)


def panel_step(current, rows_idx, cols_idx, first_tile, tile_count):
    tile_rows, tile_cols, tile_size, _ = current.shape
    width = tile_count * tile_size
    row_devices = lax.axis_size("row")
    col_devices = lax.axis_size("col")
    my_col = lax.axis_index("col")
    received = []
    for offset in range(tile_count):
        received.append(spread(current[:, 0], "col", first_tile + offset))
    panel_raw = jnp.concatenate(received, axis=2)
    diag_pieces = []
    for offset in range(tile_count):
        target = first_tile + offset
        diag_pieces.append(spread(panel_raw[target // row_devices], "row", target % row_devices))
    diag_block = jnp.concatenate(diag_pieces, axis=0)
    cholesky_factor = jnp.linalg.cholesky(diag_block)
    flattened = panel_raw.reshape(tile_rows * tile_size, width)
    solved = lax.linalg.triangular_solve(
        cholesky_factor, flattened, left_side=False, lower=True, transpose_a=True
    )
    solved = solved.reshape(tile_rows, tile_size, width)
    diag_tiles = cholesky_factor.reshape(tile_count, tile_size, width)
    row_choice = jnp.clip(rows_idx - first_tile, 0, tile_count - 1)
    diag_pick = jnp.take(diag_tiles, row_choice, axis=0)
    row_key = rows_idx[:, None, None]
    factor = jnp.where(
        row_key < first_tile, 0.0, jnp.where(row_key < first_tile + tile_count, diag_pick, solved)
    )
    gathered = []
    for column in range(tile_cols):
        target = column * col_devices + my_col
        owned_rows = lax.dynamic_index_in_dim(factor, target // row_devices, 0, keepdims=False)
        gathered.append(spread(owned_rows, "row", target % row_devices))
    across = jnp.stack(gathered)
    product = jnp.einsum("kxw,myw->kmxy", factor, across, precision=lax.Precision.HIGHEST)
    trailing = jnp.logical_and(
        rows_idx[:, None] >= first_tile + tile_count, cols_idx[None, :] >= first_tile + tile_count
    )
    in_panel = jnp.logical_and(cols_idx >= first_tile, cols_idx < first_tile + tile_count)
    col_pick = jnp.clip(cols_idx - first_tile, 0, tile_count - 1)
    panel_view = factor.reshape(tile_rows, tile_size, tile_count, tile_size)
    panel_cols = jnp.transpose(jnp.take(panel_view, col_pick, axis=2), (0, 2, 1, 3))
    updated = jnp.where(trailing[:, :, None, None], current - product, current)
    return jnp.where(in_panel[None, :, None, None], panel_cols, updated)


def on_device(covariance, tile_mask):
    tile_rows = covariance.shape[0]
    tile_cols = covariance.shape[2]
    tile_size = covariance.shape[4]
    row_devices = lax.axis_size("row")
    col_devices = lax.axis_size("col")
    my_row = lax.axis_index("row")
    my_col = lax.axis_index("col")
    rows_idx = jnp.arange(tile_rows, dtype=jnp.int32) * row_devices + my_row
    cols_idx = jnp.arange(tile_cols, dtype=jnp.int32) * col_devices + my_col
    mask_grid = tile_mask.reshape(tile_rows, row_devices, tile_cols, col_devices)
    picked = lax.dynamic_index_in_dim(mask_grid, my_row, 1, keepdims=False)
    picked = lax.dynamic_index_in_dim(picked, my_col, 2, keepdims=False)
    current = (
        covariance.reshape(tile_rows, tile_cols, tile_size, tile_size)
        * picked.astype(jnp.float32)[:, :, None, None]
    )
    for panel_index in range(PANELS):
        current = panel_step(current, rows_idx, cols_idx, panel_index * TPP, TPP)
    lead_tiles = PANELS * TPP
    above_lead = jnp.logical_and(rows_idx[:, None] < lead_tiles, cols_idx[None, :] >= lead_tiles)
    result = jnp.where(above_lead[:, :, None, None], 0.0, current).astype(jnp.bfloat16)
    return result.reshape(tile_rows, 1, tile_cols, 1, tile_size, tile_size)


def solution(mesh):
    in_specs = (P(None, "row", None, "col", None, None), P())
    out_specs = P(None, "row", None, "col", None, None)
    return jax.shard_map(
        on_device, mesh=mesh, in_specs=in_specs, out_specs=out_specs, check_vma=False
    )
```

profile of v0, /device:TPU:64, one launch (start us, length us, event | category | flops | bytes accessed | tf_op | source)
XLA Modules:
  0.0 1159.5 jit_solution(3672191470140893715)
XLA Ops:
  6.5 0.9 reshape.252
  7.7 1.4 copy.30
  9.2 0.8 select_bitcast_fusion.2
  10.1 170.7 %all-reduce.24.cloned.1.call-done = (f32[3,128,128]{1,2,0:T(8,128)}, f32[3,128,128]{1,2,0:T(8,128)}) async-done(((f32[3,128,128]{1,2,0:T(8,128)}, f32[3,128,128]{1,2,0:T(8,128)}), (f32[3,128,128]{1,2,0:T(8,128)}, f32[3,128,128]{1,2,0:T(8,128)})) %all-reduce.24.cloned.1.call-update) | async-done | bytes 393232 | tf_op jit(solution)/shard_map/psum | solution.py:12
  180.8 1.0 constant_dynamic-update-slice_fusion.1
  183.0 167.7 %all-reduce.20.cloned.1.call-done = (f32[128,256]{0,1:T(8,128)}, f32[128,256]{0,1:T(8,128)}) async-done(((f32[128,256]{0,1:T(8,128)}, f32[128,256]{0,1:T(8,128)}), (f32[128,256]{0,1:T(8,128)}, f32[128,256]{0,1:T(8,128)})) %all-reduce.20.cloned.1.call-update) | async-done | bytes 262160 | tf_op jit(solution)/shard_map/psum | solution.py:12
  350.7 0.9 constant_dynamic-update-slice_fusion.3
  351.8 11.7 %cholesky.130 = f32[128,128]{1,0:T(8,128)S(1)} custom-call(f32[128,128]{1,0:T(8,128)S(1)} %cholesky.194), custom_call_target="Cholesky" | custom-call | tf_op jit(solution)/shard_map/jit(cholesky)/cholesky | solution.py:30
  363.6 9.8 custom-call.13
  373.9 11.7 %cholesky.147 = f32[128,128]{1,0:T(8,128)S(1)} custom-call(f32[128,128]{1,0:T(8,128)S(1)} %convolution_subtract_fusion.3), custom_call_target="Cholesky" | custom-call | tf_op jit(solution)/shard_map/jit(cholesky)/cholesky | solution.py:30
  387.9 4.3 while.4
  388.7 1.4 bitcast_dynamic-update-slice_fusion.4
  390.7 1.4 bitcast_dynamic-update-slice_fusion.4
  392.2 19.7 %custom-call.14 = f32[2,128,128]{1,2,0:T(8,128)S(1)} custom-call(f32[2,128,128]{2,1,0:T(8,128)S(1)} %get-tuple-element.23), custom_call_target="InvertDiagBlocksLowerTriangular" | custom-call | tf_op jit(solution)/shard_map/triangular_solve/custom-call.0 | solution.py:32
  414.4 0.8 dynamic-slice_select_fusion.7
  416.0 166.5 %all-reduce.18.cloned.1.call-done = (f32[1,128,256]{1,2,0:T(8,128)}, f32[1,128,256]{1,2,0:T(8,128)}, f32[1,128,256]{1,2,0:T(8,128)}, f32[1,128,256]{1,2,0:T(8,128)}) async-done(((f32[1,128,256]{1,2,0:T(8,128)}, f32[1,128,256]{1,2,0:T(8,128)}, f32[1,128,256]{1,2,0:T(8,128)}, f32[1,128,256]{1,2,0:T(8,128)}), (f32[1,128,256]{1,2,0:T(8,128)}, f32[1,128,256]{1,2,0:T(8,128)}, f32[1,128,256]{1,2,0:T(8,128)}, ...) | async-done | bytes 524304 | tf_op jit(solution)/shard_map/psum | solution.py:12
  582.5 2.2 fusion.2
  585.6 161.7 %all-reduce.22.cloned.1.call-done = (f32[3,128,128]{1,2,0:T(8,128)}, f32[3,128,128]{1,2,0:T(8,128)}) async-done(((f32[3,128,128]{1,2,0:T(8,128)}, f32[3,128,128]{1,2,0:T(8,128)}), (f32[3,128,128]{1,2,0:T(8,128)}, f32[3,128,128]{1,2,0:T(8,128)})) %all-reduce.22.cloned.1.call-update) | async-done | bytes 393232 | tf_op jit(solution)/shard_map/psum | solution.py:12
  747.3 1.0 constant_dynamic-update-slice_fusion.5
  749.3 167.7 %all-reduce.16.cloned.1.call-done = (f32[128,256]{0,1:T(8,128)}, f32[128,256]{0,1:T(8,128)}) async-done(((f32[128,256]{0,1:T(8,128)}, f32[128,256]{0,1:T(8,128)}), (f32[128,256]{0,1:T(8,128)}, f32[128,256]{0,1:T(8,128)})) %all-reduce.16.cloned.1.call-update) | async-done | bytes 262160 | tf_op jit(solution)/shard_map/psum | solution.py:12
  917.0 0.9 constant_dynamic-update-slice_fusion.7
  918.2 11.7 %cholesky.164 = f32[128,128]{1,0:T(8,128)S(1)} custom-call(f32[128,128]{1,0:T(8,128)S(1)} %cholesky.197), custom_call_target="Cholesky" | custom-call | tf_op jit(solution)/shard_map/jit(cholesky)/cholesky | solution.py:30
  929.9 9.8 custom-call.15
  940.2 11.7 %cholesky.181 = f32[128,128]{1,0:T(8,128)S(1)} custom-call(f32[128,128]{1,0:T(8,128)S(1)} %convolution_subtract_fusion.2), custom_call_target="Cholesky" | custom-call | tf_op jit(solution)/shard_map/jit(cholesky)/cholesky | solution.py:30
  954.7 4.3 while.5
  955.6 1.4 bitcast_dynamic-update-slice_fusion.5
  957.6 1.4 bitcast_dynamic-update-slice_fusion.5
  959.1 19.7 %custom-call.16 = f32[2,128,128]{1,2,0:T(8,128)S(1)} custom-call(f32[2,128,128]{2,1,0:T(8,128)S(1)} %get-tuple-element.24), custom_call_target="InvertDiagBlocksLowerTriangular" | custom-call | tf_op jit(solution)/shard_map/triangular_solve/custom-call.0 | solution.py:32
  981.3 0.8 dynamic-slice_select_fusion.3
  982.9 166.6 %all-reduce.14.cloned.1.call-done = (f32[1,128,256]{1,2,0:T(8,128)}, f32[1,128,256]{1,2,0:T(8,128)}, f32[1,128,256]{1,2,0:T(8,128)}, f32[1,128,256]{1,2,0:T(8,128)}) async-done(((f32[1,128,256]{1,2,0:T(8,128)}, f32[1,128,256]{1,2,0:T(8,128)}, f32[1,128,256]{1,2,0:T(8,128)}, f32[1,128,256]{1,2,0:T(8,128)}), (f32[1,128,256]{1,2,0:T(8,128)}, f32[1,128,256]{1,2,0:T(8,128)}, f32[1,128,256]{1,2,0:T(8,128)}, ...) | async-done | bytes 524304 | tf_op jit(solution)/shard_map/psum | solution.py:12
  1149.4 2.3 fusion.8
  1151.7 0.9 copy.46
  (101 shorter events, 15.8 us)
Async XLA Ops:
  6.5 174.3 %all-reduce.24.cloned.1.call-start = ((), (), s32[]{:S(2)}) async-start(), calls=%async_computation.5 | async-start | bytes 786432 | tf_op jit(solution)/shard_map/psum | solution.py:12
  10.0 340.7 %all-reduce.20.cloned.1.call-start = ((), (), s32[]{:S(2)}) async-start(), calls=%async_computation.3 | async-start | bytes 524288 | tf_op jit(solution)/shard_map/psum | solution.py:12
  180.8 1.0 copy-start
  182.6 399.9 %all-reduce.18.cloned.1.call-start = ((), (), s32[]{:S(2)}) async-start(), calls=%async_computation.2 | async-start | bytes 1048576 | tf_op jit(solution)/shard_map/psum | solution.py:12
  350.7 1.0 copy-start.2
  415.2 332.1 %all-reduce.22.cloned.1.call-start = ((), (), s32[]{:S(2)}) async-start(), calls=%async_computation.4 | async-start | bytes 786432 | tf_op jit(solution)/shard_map/psum | solution.py:12
  585.5 331.5 %all-reduce.16.cloned.1.call-start = ((), (), s32[]{:S(2)}) async-start(), calls=%async_computation.1 | async-start | bytes 524288 | tf_op jit(solution)/shard_map/psum | solution.py:12
  747.3 1.0 copy-start.1
  749.1 400.4 %all-reduce.14.cloned.1.call-start = ((), (), s32[]{:S(2)}) async-start(), calls=%async_computation | async-start | bytes 1048576 | tf_op jit(solution)/shard_map/psum | solution.py:12
  917.0 1.0 copy-start.3
Sparse Core Ops, SparseCore 0:
  10.1 170.6 all-reduce.23
  184.7 165.8 all-reduce.19
  415.3 167.1 all-reduce.17
  585.6 161.6 all-reduce.21
  751.0 165.9 all-reduce.15
  982.3 167.1 all-reduce.13
where the time goes:
time: 1160 us
  waiting for transfers between devices  1000 us (86%)
  other arithmetic  113 us (10%)
  local copies, waits for them, and re-layouts  19.5 us (2%)
  between operations  16.8 us (1%)
    psum x6, waiting for transfers between devices, spread(): return lax.psum(kept, axis)  1000 us
    another operation x13, other arithmetic, panel_step(): cholesky_factor = jnp.linalg.cholesky(diag_block)  68.7 us
    another operation x7, other arithmetic, panel_step(): lax.linalg.triangular_solve(cholesky_factor, flattened, left_side=False,...  39.5 us
  transfers between devices with their start and end apart: 6, of which 6 were waited for; matrix products, arithmetic and copies ran while one was open for 0% of the time, Pallas kernels for 0%

commit v1 on v0

v1 whole, which is shorter than its diff:
```python
import functools

import jax
import jax.numpy as jnp
from jax import lax
from jax.experimental import pallas as pl
from jax.experimental.pallas import tpu as pltpu
from jax.sharding import PartitionSpec as P

MESH = pl.DeviceIdType.MESH
f32 = jnp.float32
NN = (((1,), (0,)), ((), ()))
NT = (((1,), (1,)), ((), ()))
TN = (((0,), (0,)), ((), ()))
NX = 4
NY = 8
NZ = 12
LEAD_TILES = 4
SEND_SEMS = 120


def dot(a, b, dims=NN):
    return lax.dot_general(
        a, b, dims, precision=lax.Precision.HIGHEST, preferred_element_type=f32
    )


class Spread:
    def __init__(self, lead, rows, cols, recv, sent):
        self.lead, self.rows, self.cols, self.recv, self.sent = lead, rows, cols, recv, sent
        row = lax.axis_index("row")
        col = lax.axis_index("col")
        self.y, self.x = row // NX, row % NX
        self.z, self.q = col // 2, col % 2
        self.started = []

    def device(self, dx=0, dy=0, dz=0, dq=0):
        x = (self.x + dx) % NX
        y = (self.y + dy + NY) % NY
        z = (self.z + dz + NZ) % NZ
        q = 1 - self.q if dq else self.q
        return (y * NX + x, z * 2 + q)

    def barrier(self):
        sem = pltpu.get_barrier_semaphore()
        peers = [self.device(dx=d) for d in (1, 2, 3)]
        peers += [self.device(dy=d) for d in (1, -1)]
        peers += [self.device(dz=d) for d in (1, -1)]
        peers += [self.device(dq=1)]
        for peer in peers:
            pl.semaphore_signal(sem, inc=1, device_id=peer, device_id_type=MESH)
        pl.semaphore_wait(sem, len(peers))

    def send(self, cond, slot, device):
        ref, sem = slot
        copy = pltpu.make_async_remote_copy(
            src_ref=ref,
            dst_ref=ref,
            send_sem=self.sent.at[len(self.started)],
            recv_sem=sem,
            device_id=device,
            device_id_type=MESH,
        )

        @pl.when(cond)
        def _():
            copy.start()

        self.started.append((cond, copy))

    def arrive(self, cond, slot):
        ref, sem = slot
        copy = pltpu.make_async_copy(ref, ref, sem)

        @pl.when(cond)
        def _():
            copy.wait()

    def finish(self):
        for cond, copy in self.started:

            @pl.when(cond)
            def _():
                copy.wait_send()

    def lead_slot(self, i, k):
        return self.lead.at[i, k], self.recv.at[i * 4 + k]

    def row_slot(self, k, a):
        return self.rows.at[k, a], self.recv.at[16 + k * 3 + a]

    def col_slot(self, k, b):
        return self.cols.at[k, b], self.recv.at[28 + k * 4 + b]


def spread_tiles(net, cov):
    x, y, z, q = net.x, net.y, net.z, net.q
    always = y >= 0
    top = y == 0
    y_up = y <= 3
    y_down = jnp.logical_or(y == 0, y >= 6)

    @pl.when(top)
    def _():
        for zs in range(2):
            k = q + 2 * zs

            @pl.when(jnp.logical_and(z == zs, x >= k))
            def _():
                ref, sem = net.lead_slot(x, k)
                pltpu.make_async_copy(cov.at[0, 0, 0, 0], ref, sem).start()

        for b in range(4):
            ref, sem = net.col_slot(x, b)
            pltpu.make_async_copy(cov.at[0, 0, b, 0], ref, sem).start()

    for zs in range(2):

        @pl.when(z == zs)
        def _():
            for a in range(3):
                ref, sem = net.row_slot(q + 2 * zs, a)
                pltpu.make_async_copy(cov.at[a, 0, 0, 0], ref, sem).start()

    net.barrier()

    def along_z(cond, zs, slot):
        rel = (z - zs + NZ) % NZ
        net.send(jnp.logical_and(cond, rel <= 5), slot, net.device(dz=1))
        down = jnp.logical_or(rel == 0, rel >= 8)
        net.send(jnp.logical_and(cond, down), slot, net.device(dz=-1))

    def along_y(cond, slot):
        net.send(jnp.logical_and(cond, y_up), slot, net.device(dy=1))
        net.send(jnp.logical_and(cond, y_down), slot, net.device(dy=-1))

    def along_x(cond, slot):
        for dx in (1, 3, 2):
            net.send(cond, slot, net.device(dx=dx))

    def to_partner(cond, slot):
        net.send(cond, slot, net.device(dq=1))

    def rows(zs, a):
        slot = net.row_slot(q + 2 * zs, a)
        net.arrive(always, slot)
        along_z(always, zs, slot)
        to_partner(always, slot)

    def cols(b):
        slot = net.col_slot(x, b)
        net.arrive(always, slot)
        along_y(always, slot)
        along_x(always, slot)

    for zs in range(2):
        k = q + 2 * zs
        slot = net.lead_slot(x, k)
        cond = jnp.logical_and(top, x >= k)
        net.arrive(cond, slot)
        along_z(cond, zs, slot)
        along_y(cond, slot)
        along_x(cond, slot)
        to_partner(cond, slot)
    rows(0, 0)
    rows(1, 0)
    cols(0)
    rows(0, 1)
    rows(1, 1)
    cols(1)
    rows(0, 2)
    rows(1, 2)
    cols(2)
    cols(3)
    for zs in range(2):
        k = q + 2 * zs
        slot = net.lead_slot(x, k)
        cond = jnp.logical_and(y != 0, x >= k)
        net.arrive(cond, slot)
        along_y(cond, slot)
        along_x(cond, slot)
        to_partner(cond, slot)
    for zs in range(2):
        for dx in (1, 3, 2):
            i = (x + dx) % NX
            k = q + 2 * zs
            slot = net.lead_slot(i, k)
            net.arrive(i >= k, slot)
            to_partner(i >= k, slot)
    for zs in range(2):
        for i in range(LEAD_TILES):
            k = 1 - q + 2 * zs
            net.arrive(i >= k, net.lead_slot(i, k))
    for dx in (1, 3, 2):
        for b in range(4):
            net.arrive(always, net.col_slot((x + dx) % NX, b))
    for zs in range(2):
        for a in range(3):
            net.arrive(always, net.row_slot(1 - q + 2 * zs, a))
    net.finish()


def factor_tile(work):
    sub = lax.broadcasted_iota(jnp.int32, (8, 128), 0)

    def across(value, k):
        return jnp.broadcast_to(value[k : k + 1, :], (8, 128))

    def along(value, k):
        return jnp.broadcast_to(value[:, k : k + 1], (8, 128))

    for block in range(16):
        r0 = 8 * block
        last = block == 15
        xa = work[r0 : r0 + 8, 0:128]
        xe = work[r0 : r0 + 8, 128:256]
        here = [along(xa, r0 + k) for k in range(8)]
        if not last:
            na = work[r0 + 8 : r0 + 16, 0:128]
            ne = work[r0 + 8 : r0 + 16, 128:256]
            below = [along(na, r0 + k) for k in range(8)]
        pivots = jnp.ones((8, 128), f32)
        for k in range(8):
            pivot = across(here[k], k)
            inverse = 1.0 / pivot
            ra = across(xa, k)
            re = across(xe, k)
            m = jnp.where(sub > k, here[k] * inverse, 0.0)
            pivots = jnp.where(sub == k, pivot, pivots)
            if not last:
                n = below[k] * inverse
            for j in range(k + 1, 8):
                entry = across(here[j], k)
                here[j] = here[j] - m * entry
                if not last:
                    below[j] = below[j] - n * entry
            xa = xa - m * ra
            xe = xe - m * re
            if not last:
                na = na - n * ra
                ne = ne - n * re
        scale = lax.rsqrt(pivots)
        ua = xa * scale
        ue = xe * scale
        work[r0 : r0 + 8, 0:128] = ua
        work[r0 : r0 + 8, 128:256] = ue
        if not last:
            work[r0 + 8 : r0 + 16, 0:128] = na
            work[r0 + 8 : r0 + 16, 128:256] = ne
        if block < 14:
            q0 = r0 + 16
            update = dot(ua, jnp.concatenate([ua, ue], axis=1), TN)
            work[q0:, :] = work[q0:, :] - update[q0:, :]


def kernel(mask, cov, out, lead, rows, cols, own, work, left, right, recv, sent, own_sem):
    r = lax.axis_index("row")
    c = lax.axis_index("col")
    own_copy = pltpu.make_async_copy(cov.at[:, 0, :, 0], own, own_sem)
    own_copy.start()
    spread_tiles(Spread(lead, rows, cols, recv, sent), cov)
    across = lax.broadcasted_iota(jnp.int32, (128, 128), 1)
    down = lax.broadcasted_iota(jnp.int32, (128, 128), 0)
    eye = (across == down).astype(f32)
    for k in range(LEAD_TILES):
        here = slice(128 * k, 128 * k + 128)
        work[:, 0:128] = lead[k, k]
        work[:, 128:256] = eye
        factor_tile(work)
        inverse = work[:, 128:256]
        for i in range(k + 1, LEAD_TILES):
            lead[i, k] = dot(lead[i, k], inverse, NT)
        for i in range(k + 1, LEAD_TILES):
            for j in range(k + 1, i + 1):
                lead[i, j] = lead[i, j] - dot(lead[i, k], lead[j, k], NT)
        raw = jnp.concatenate(
            [cols[k, b] * mask[k, b * 24 + c].astype(f32) for b in range(4)], axis=1
        )
        for j in range(k):
            raw = raw - dot(lead[k, j], right[128 * j : 128 * j + 128, :])
        right[here, :] = dot(inverse, raw)
        for a in range(3):
            raw = rows[k, a] * mask[a * 32 + r, k].astype(f32)
            for j in range(k):
                raw = raw - dot(left[a, :, 128 * j : 128 * j + 128], lead[k, j], NT)
            left[a, :, here] = dot(raw, inverse, NT)
    own_copy.wait()
    pick = pl.ds(pl.multiple_of(jnp.minimum(c, 3) * 128, 128), 128)
    for a in range(3):
        tile_row = a * 32 + r
        product = dot(left[a], right[...])
        for b in range(4):
            masked = own[a, b] * mask[tile_row, b * 24 + c].astype(f32)
            value = masked - product[:, 128 * b : 128 * b + 128]
            if a == 0:
                value = jnp.where(r < LEAD_TILES, 0.0, value)
            if b == 0:
                lower = (tile_row - c) * 128 + down >= across
                value = jnp.where(c < LEAD_TILES, jnp.where(lower, left[a, :, pick], 0.0), value)
            out[a, 0, b, 0] = value.astype(jnp.bfloat16)


def on_device(covariance, tile_mask):
    vmem = pltpu.VMEM
    return pl.pallas_call(
        kernel,
        out_shape=jax.ShapeDtypeStruct(covariance.shape, jnp.bfloat16),
        in_specs=[pl.BlockSpec(memory_space=pltpu.SMEM), pl.BlockSpec(memory_space=pl.ANY)],
        out_specs=pl.BlockSpec(memory_space=vmem),
        scratch_shapes=[
            vmem((4, 4, 128, 128), f32),
            vmem((4, 3, 128, 128), f32),
            vmem((4, 4, 128, 128), f32),
            vmem((3, 4, 128, 128), f32),
            vmem((128, 256), f32),
            vmem((3, 128, 512), f32),
            vmem((512, 512), f32),
            pltpu.SemaphoreType.DMA((44,)),
            pltpu.SemaphoreType.DMA((SEND_SEMS,)),
            pltpu.SemaphoreType.DMA,
        ],
        compiler_params=pltpu.CompilerParams(collective_id=0, has_side_effects=True),
        name="panels",
    )(tile_mask, covariance)


def solution(mesh):
    in_specs = (P(None, "row", None, "col", None, None), P())
    out_specs = P(None, "row", None, "col", None, None)
    return jax.shard_map(
        on_device, mesh=mesh, in_specs=in_specs, out_specs=out_specs, check_vma=False
    )
```

time: 1160 us -> 108 us (0.09)
  the two profiles are of different devices: /device:TPU:64 before, /device:TPU:481 now
where the time goes in v1:
time: 108 us
  Pallas kernels  106 us (98%)
  local copies, waits for them, and re-layouts  1.77 us (2%)
    pallas_call x1, Pallas kernels, on_device(): pl.pallas_call(kernel, out_shape=jax.ShapeDtypeStruct(covariance.shape, j...  106 us

profile of v1, /device:TPU:481, one launch (start us, length us, event | category | flops | bytes accessed | tf_op | source)
XLA Modules:
  0.0 108.1 jit_solution(5856235532546389402)
XLA Ops:
  0.0 106.3 %panels.1 = bf16[3,1,4,1,128,128]{5,4,3,2,1,0:T(8,128)(2,1)} custom-call(s32[96,96]{1,0:T(8,128)} %mask.1, f32[3,1,4,1,128,128]{5,4,3,2,1,0:T(8,128)} %cov.1), custom_call_target="tpu_custom_call" | custom-call | tf_op jit(solution)/shard_map/panels/pallas_call | solution.py:305
  106.3 1.8 %copy.4 = bf16[3,1,4,1,128,128]{5,4,3,2,1,0:T(8,128)(2,1)} copy(bf16[3,1,4,1,128,128]{5,4,3,2,1,0:T(8,128)(2,1)} %panels.1) | data formatting | bytes 786432

commit v2 on v0

v2 whole, which is shorter than its diff:
```python
import functools

import jax
import jax.numpy as jnp
from jax import lax
from jax.experimental import pallas as pl
from jax.experimental.pallas import tpu as pltpu
from jax.sharding import PartitionSpec as P

MESH = pl.DeviceIdType.MESH
f32 = jnp.float32
NN = (((1,), (0,)), ((), ()))
NT = (((1,), (1,)), ((), ()))
TN = (((0,), (0,)), ((), ()))
NX = 4
NY = 8
NZ = 12
LEAD_TILES = 4
PIECE = 16


def dot(a, b, dims=NN):
    return lax.dot_general(
        a, b, dims, precision=lax.Precision.HIGHEST, preferred_element_type=f32
    )


def factor_tile(work):
    sub = lax.broadcasted_iota(jnp.int32, (8, 128), 0)

    def across(value, k):
        return jnp.broadcast_to(value[k : k + 1, :], (8, 128))

    def along(value, k):
        return jnp.broadcast_to(value[:, k : k + 1], (8, 128))

    for block in range(16):
        r0 = 8 * block
        last = block == 15
        xa = work[r0 : r0 + 8, 0:128]
        xe = work[r0 : r0 + 8, 128:256]
        here = [along(xa, r0 + k) for k in range(8)]
        if not last:
            na = work[r0 + 8 : r0 + 16, 0:128]
            ne = work[r0 + 8 : r0 + 16, 128:256]
            below = [along(na, r0 + k) for k in range(8)]
        pivots = jnp.ones((8, 128), f32)
        for k in range(8):
            pivot = across(here[k], k)
            inverse = 1.0 / pivot
            ra = across(xa, k)
            re = across(xe, k)
            m = jnp.where(sub > k, here[k] * inverse, 0.0)
            pivots = jnp.where(sub == k, pivot, pivots)
            if not last:
                n = below[k] * inverse
            for j in range(k + 1, 8):
                entry = across(here[j], k)
                here[j] = here[j] - m * entry
                if not last:
                    below[j] = below[j] - n * entry
            xa = xa - m * ra
            xe = xe - m * re
            if not last:
                na = na - n * ra
                ne = ne - n * re
        scale = lax.rsqrt(pivots)
        ua = xa * scale
        ue = xe * scale
        work[r0 : r0 + 8, 0:128] = ua
        work[r0 : r0 + 8, 128:256] = ue
        if not last:
            work[r0 + 8 : r0 + 16, 0:128] = na
            work[r0 + 8 : r0 + 16, 128:256] = ne
        if block < 14:
            q0 = r0 + 16
            update = dot(ua, jnp.concatenate([ua, ue], axis=1), TN)
            work[q0:, :] = work[q0:, :] - update[q0:, :]


class Net:
    def __init__(self, recv, sent):
        self.recv, self.sent = recv, sent
        row = lax.axis_index("row")
        col = lax.axis_index("col")
        self.y, self.x = row // NX, row % NX
        self.z, self.q = col // 2, col % 2
        self.started = []
        self.slots = {}
        self.arrivals = {}

    def device(self, dx=0, dy=0, dz=0, dq=0):
        x = (self.x + dx) % NX
        y = (self.y + dy + NY) % NY
        z = (self.z + dz + NZ) % NZ
        q = (self.q + dq) % 2
        return (y * NX + x, z * 2 + q)

    def group(self):
        return [
            self.device(dx=dx, dq=dq) for dx in (2, 1, 3, 0) for dq in (0, 1) if dx or dq
        ]

    def column(self):
        return [self.device(dy=dy) for dy in (4, 3, -3, 2, -2, 1, -1)]

    def ring(self):
        return [self.device(dz=dz) for dz in (6, 5, -5, 4, -4, 3, -3, 2, -2, 1, -1)]

    def barrier(self):
        sem = pltpu.get_barrier_semaphore()
        peers = self.ring() + self.column() + self.group()
        for peer in peers:
            pl.semaphore_signal(sem, inc=1, device_id=peer, device_id_type=MESH)
        pl.semaphore_wait(sem, len(peers))

    def send(self, cond, key, slot, device):
        ref, sem = slot
        index = self.slots.setdefault(key, len(self.slots))
        copy = pltpu.make_async_remote_copy(
            src_ref=ref,
            dst_ref=ref,
            send_sem=self.sent.at[index],
            recv_sem=self.recv.at[sem],
            device_id=device,
            device_id_type=MESH,
        )

        @pl.when(cond)
        def _():
            copy.start()

        self.started.append((cond, copy))

    def load(self, cond, source, slot):
        ref, sem = slot

        @pl.when(cond)
        def _():
            pltpu.make_async_copy(source, ref, self.recv.at[sem]).start()

    def arrive(self, cond, slot):
        ref, sem = slot

        @pl.when(cond)
        def _():
            pltpu.make_async_copy(ref, ref, self.recv.at[sem]).wait()

    def finish(self):
        for cond, copy in self.started:

            @pl.when(cond)
            def _():
                copy.wait_send()


RAW_SEM, ROW_SEM, COL_SEM, PIECE_SEM = 0, 16, 28, 44
RECV_SEMS = 76
SEND_SEMS = 125


def kernel(
    mask, cov, out, raw, trail, factor, rows, cols, own, work, left, right, schur, recv, sent,
    own_sem,
):
    r = lax.axis_index("row")
    c = lax.axis_index("col")
    net = Net(recv, sent)
    x, y, z, q = net.x, net.y, net.z, net.q
    both = jnp.logical_and
    always = y >= 0
    top = y == 0
    factors = both(top, z == 0)
    relays = jnp.logical_not(factors)
    own_copy = pltpu.make_async_copy(cov.at[:, 0, :, 0], own, own_sem)
    piece_of = x * 2 + q

    def raw_slot(i, k):
        return raw.at[i, k], RAW_SEM + i * 4 + k

    def row_slot(k, a):
        return rows.at[k, a], ROW_SEM + k * 3 + a

    def col_slot(k, b):
        return cols.at[k, b], COL_SEM + k * 4 + b

    def piece_slot(k, piece):
        span = pl.ds(pl.multiple_of(piece * PIECE, PIECE), PIECE)
        return factor.at[k, pl.ds(0, 4 - k), span], PIECE_SEM + k * 8 + piece

    near = both(factors, x >= q)
    far = both(both(top, z == 1), x >= q + 2)
    net.load(near, cov.at[0, 0, 0, 0], raw_slot(x, q))
    net.load(far, cov.at[0, 0, 0, 0], raw_slot(x, q + 2))
    for b in range(4):
        net.load(top, cov.at[0, 0, b, 0], col_slot(x, b))
    for zs in range(2):
        for a in range(3):
            net.load(z == zs, cov.at[a, 0, 0, 0], row_slot(q + 2 * zs, a))
    own_copy.start()
    net.barrier()

    def send_raw(cond, k, tag):
        slot = raw_slot(x, k)
        net.arrive(cond, slot)
        for n, peer in enumerate(net.group()):
            net.send(cond, ("raw", tag, n), slot, peer)

    def send_rows(cond, zs, a):
        slot = row_slot(q + 2 * zs, a)
        net.arrive(cond, slot)
        rel = (z - zs + NZ) % NZ
        up = rel <= 5
        down = jnp.logical_or(rel == 0, rel >= 8)
        net.send(both(cond, up), ("row", zs, a, 0), slot, net.device(dz=1))
        net.send(both(cond, down), ("row", zs, a, 1), slot, net.device(dz=-1))
        net.send(cond, ("row", zs, a, 2), slot, net.device(dq=1))

    def send_cols(cond, b):
        slot = col_slot(x, b)
        net.arrive(cond, slot)
        up = y <= 3
        down = jnp.logical_or(y == 0, y >= 6)
        net.send(both(cond, up), ("col", b, 0), slot, net.device(dy=1))
        net.send(both(cond, down), ("col", b, 1), slot, net.device(dy=-1))
        for dx in range(1, NX):
            net.send(cond, ("col", b, 1 + dx), slot, net.device(dx=dx))

    send_raw(near, q, 0)
    net.arrive(far, raw_slot(x, q + 2))
    net.send(far, ("raw", 1, 7), raw_slot(x, q + 2), net.device(dz=-1))
    passed = both(factors, x >= q + 2)
    send_raw(passed, q + 2, 1)
    for a in range(3):
        for zs in range(2):
            send_rows(z == zs, zs, a)
    for b in range(4):
        send_cols(top, b)

    across = lax.broadcasted_iota(jnp.int32, (128, 128), 1)
    down = lax.broadcasted_iota(jnp.int32, (128, 128), 0)

    def raw_arrive(i, k):
        net.arrive(both(factors, both(jnp.logical_or(x != i, q != k % 2), True)), raw_slot(i, k))

    for k in range(LEAD_TILES):
        if k == 0:
            raw_arrive(0, 0)

        @pl.when(factors)
        def _():
            work[:, 0:128] = raw[0, 0] if k == 0 else trail[k, k]
            work[:, 128:256] = (across == down).astype(f32)
            factor_tile(work)
            factor[k, 0] = work[:, 128:256]

        if k == 0:
            for i in range(1, LEAD_TILES):
                raw_arrive(i, 0)

        @pl.when(factors)
        def _():
            for i in range(k + 1, LEAD_TILES):
                tile = raw[i, 0] if k == 0 else trail[i, k]
                factor[k, i - k] = dot(tile, work[:, 128:256], NT)

        slot = piece_slot(k, piece_of)
        for n, peer in enumerate(net.ring() + net.column()):
            net.send(factors, ("piece", k, n), slot, peer)
        if k == 0:
            for i in range(1, LEAD_TILES):
                for j in range(1, i + 1):
                    raw_arrive(i, j)

        @pl.when(factors)
        def _():
            for i in range(k + 1, LEAD_TILES):
                for j in range(k + 1, i + 1):
                    old = raw[i, j] if k == 0 else trail[i, j]
                    trail[i, j] = old - dot(factor[k, i - k], factor[k, j - k], NT)

        if k == 0:
            for a in range(3):
                send_rows(factors, 1, a)

    for a in range(3):
        for zs in range(2):
            send_rows(both(relays, z != zs), zs, a)
        send_cols(jnp.logical_not(top), a)
    send_cols(jnp.logical_not(top), 3)
    for dx in range(1, NX):
        for b in range(4):
            net.arrive(always, col_slot((x + dx) % NX, b))
    for zs in range(2):
        for a in range(3):
            net.arrive(always, row_slot(1 - q + 2 * zs, a))
    for k in range(LEAD_TILES):
        for b in range(4):
            right[k, :, 128 * b : 128 * b + 128] = cols[k, b] * mask[k, b * 24 + c].astype(f32)
        for a in range(3):
            left[k, 128 * a : 128 * a + 128, :] = rows[k, a] * mask[a * 32 + r, k].astype(f32)
    own_copy.wait()
    for a in range(3):
        for b in range(4):
            schur[128 * a : 128 * a + 128, 128 * b : 128 * b + 128] = own[a, b] * mask[
                a * 32 + r, b * 24 + c
            ].astype(f32)

    passing = both(relays, top)
    for k in range(LEAD_TILES):
        slot = piece_slot(k, piece_of)
        net.arrive(relays, slot)
        for n, peer in enumerate(net.column()):
            net.send(passing, ("piece", k, 11 + n), slot, peer)
        for n, peer in enumerate(net.group()):
            net.send(relays, ("piece", k, n), slot, peer)
        for n in range(1, 8):
            net.arrive(relays, piece_slot(k, (piece_of + n) % 8))
        inverse = factor[k, 0]
        zk = dot(inverse, right[k])
        yk = dot(left[k], inverse, NT)
        left[k] = yk
        for i in range(k + 1, LEAD_TILES):
            lower = factor[k, i - k]
            right[i] = right[i] - dot(lower, zk)
            left[i] = left[i] - dot(yk, lower, NT)
        schur[...] = schur[...] - dot(yk, zk)

    edge = jnp.minimum(c, 3)
    for a in range(3):
        tile_row = a * 32 + r
        for b in range(4):
            value = schur[128 * a : 128 * a + 128, 128 * b : 128 * b + 128]
            if a == 0:
                value = jnp.where(r < LEAD_TILES, 0.0, value)
            if b == 0:
                lower = (tile_row - c) * 128 + down >= across
                column = jnp.where(lower, left[edge, 128 * a : 128 * a + 128, :], 0.0)
                value = jnp.where(c < LEAD_TILES, column, value)
            out[a, 0, b, 0] = value.astype(jnp.bfloat16)
    net.finish()


def on_device(covariance, tile_mask):
    vmem = pltpu.VMEM
    return pl.pallas_call(
        kernel,
        out_shape=jax.ShapeDtypeStruct(covariance.shape, jnp.bfloat16),
        in_specs=[pl.BlockSpec(memory_space=pltpu.SMEM), pl.BlockSpec(memory_space=pl.ANY)],
        out_specs=pl.BlockSpec(memory_space=vmem),
        scratch_shapes=[
            vmem((4, 4, 128, 128), f32),
            vmem((4, 4, 128, 128), f32),
            vmem((4, 4, 128, 128), f32),
            vmem((4, 3, 128, 128), f32),
            vmem((4, 4, 128, 128), f32),
            vmem((3, 4, 128, 128), f32),
            vmem((128, 256), f32),
            vmem((4, 384, 128), f32),
            vmem((4, 128, 512), f32),
            vmem((384, 512), f32),
            pltpu.SemaphoreType.DMA((RECV_SEMS,)),
            pltpu.SemaphoreType.DMA((SEND_SEMS,)),
            pltpu.SemaphoreType.DMA,
        ],
        compiler_params=pltpu.CompilerParams(collective_id=0, has_side_effects=True),
        name="panels",
    )(tile_mask, covariance)


def solution(mesh):
    in_specs = (P(None, "row", None, "col", None, None), P())
    out_specs = P(None, "row", None, "col", None, None)
    return jax.shard_map(
        on_device, mesh=mesh, in_specs=in_specs, out_specs=out_specs, check_vma=False
    )
```

time: 1160 us -> 83 us (0.07)
  the two profiles are of different devices: /device:TPU:64 before, /device:TPU:457 now
where the time goes in v2:
time: 83 us; the launch traced here: 82.8 us
  Pallas kernels  81 us (98%)
  local copies, waits for them, and re-layouts  1.77 us (2%)
    pallas_call x1, Pallas kernels, on_device(): pl.pallas_call(kernel, out_shape=jax.ShapeDtypeStruct(covariance.shape, j...  81 us
    unnamed x1, local copies, waits for them, and re-layouts  1.77 us

profile of v2, /device:TPU:457, one launch (start us, length us, event | category | flops | bytes accessed | tf_op | source)
XLA Modules:
  0.0 82.8 jit_solution(2542421184784362727)
XLA Ops:
  0.0 81.0 %panels.1 = bf16[3,1,4,1,128,128]{5,4,3,2,1,0:T(8,128)(2,1)} custom-call(s32[96,96]{1,0:T(8,128)} %mask.1, f32[3,1,4,1,128,128]{5,4,3,2,1,0:T(8,128)} %cov.1), custom_call_target="tpu_custom_call" | custom-call | tf_op jit(solution)/shard_map/panels/pallas_call | solution.py:346
  81.0 1.8 %copy.4 = bf16[3,1,4,1,128,128]{5,4,3,2,1,0:T(8,128)(2,1)} copy(bf16[3,1,4,1,128,128]{5,4,3,2,1,0:T(8,128)(2,1)} %panels.1) | data formatting | bytes 786432

commit v3 on v2

--- a/solution.py
+++ b/solution.py
@@ -34,48 +34,43 @@
     def along(value, k):
         return jnp.broadcast_to(value[:, k : k + 1], (8, 128))
 
-    for block in range(16):
-        r0 = 8 * block
-        last = block == 15
-        xa = work[r0 : r0 + 8, 0:128]
-        xe = work[r0 : r0 + 8, 128:256]
-        here = [along(xa, r0 + k) for k in range(8)]
-        if not last:
-            na = work[r0 + 8 : r0 + 16, 0:128]
-            ne = work[r0 + 8 : r0 + 16, 128:256]
-            below = [along(na, r0 + k) for k in range(8)]
-        pivots = jnp.ones((8, 128), f32)
-        for k in range(8):
-            pivot = across(here[k], k)
-            inverse = 1.0 / pivot
-            ra = across(xa, k)
-            re = across(xe, k)
-            m = jnp.where(sub > k, here[k] * inverse, 0.0)
-            pivots = jnp.where(sub == k, pivot, pivots)
-            if not last:
-                n = below[k] * inverse
-            for j in range(k + 1, 8):
-                entry = across(here[j], k)
-                here[j] = here[j] - m * entry
-                if not last:
-                    below[j] = below[j] - n * entry
-            xa = xa - m * ra
-            xe = xe - m * re
-            if not last:
-                na = na - n * ra
-                ne = ne - n * re
-        scale = lax.rsqrt(pivots)
-        ua = xa * scale
-        ue = xe * scale
-        work[r0 : r0 + 8, 0:128] = ua
-        work[r0 : r0 + 8, 128:256] = ue
-        if not last:
-            work[r0 + 8 : r0 + 16, 0:128] = na
-            work[r0 + 8 : r0 + 16, 128:256] = ne
-        if block < 14:
-            q0 = r0 + 16
-            update = dot(ua, jnp.concatenate([ua, ue], axis=1), TN)
-            work[q0:, :] = work[q0:, :] - update[q0:, :]
+    for group in range(4):
+        q0 = 32 * group
+        xa = [work[q0 + 8 * i : q0 + 8 * i + 8, 0:128] for i in range(4)]
+        xe = [work[q0 + 8 * i : q0 + 8 * i + 8, 128:256] for i in range(4)]
+        for block in range(4):
+            live = range(block, 4)
+            heads = {i: [along(xa[i], q0 + 8 * block + k) for k in range(8)] for i in live}
+            pivots = jnp.ones((8, 128), f32)
+            for k in range(8):
+                pivot = across(heads[block][k], k)
+                inverse = 1.0 / pivot
+                ra = across(xa[block], k)
+                re = across(xe[block], k)
+                pivots = jnp.where(sub == k, pivot, pivots)
+                m = {i: heads[i][k] * inverse for i in live}
+                m[block] = jnp.where(sub > k, m[block], 0.0)
+                for j in range(k + 1, 8):
+                    entry = across(heads[block][j], k)
+                    for i in live:
+                        heads[i][j] = heads[i][j] - m[i] * entry
+                for i in live:
+                    xa[i] = xa[i] - m[i] * ra
+                    xe[i] = xe[i] - m[i] * re
+            scale = lax.rsqrt(pivots)
+            xa[block] = xa[block] * scale
+            xe[block] = xe[block] * scale
+            r0 = q0 + 8 * block
+            work[r0 : r0 + 8, 0:128] = xa[block]
+            work[r0 : r0 + 8, 128:256] = xe[block]
+        if group < 3:
+            upper = jnp.concatenate(xa, axis=0)
+            both = jnp.concatenate([upper, jnp.concatenate(xe, axis=0)], axis=1)
+            turned = upper.T
+            q1, q2 = q0 + 32, q0 + 64
+            work[q1:q2, :] = work[q1:q2, :] - dot(turned[q1:q2, :], both)
+            if group < 2:
+                work[q2:, :] = work[q2:, :] - dot(turned[q2:, :], both)
 
 
 class Net:
@@ -216,26 +211,31 @@
         net.send(both(cond, down), ("row", zs, a, 1), slot, net.device(dz=-1))
         net.send(cond, ("row", zs, a, 2), slot, net.device(dq=1))
 
-    def send_cols(cond, b):
+    def cols_along_y(cond, b):
         slot = col_slot(x, b)
         net.arrive(cond, slot)
         up = y <= 3
         down = jnp.logical_or(y == 0, y >= 6)
         net.send(both(cond, up), ("col", b, 0), slot, net.device(dy=1))
         net.send(both(cond, down), ("col", b, 1), slot, net.device(dy=-1))
+
+    def cols_along_x(cond, b):
+        slot = col_slot(x, b)
         for dx in range(1, NX):
             net.send(cond, ("col", b, 1 + dx), slot, net.device(dx=dx))
 
     send_raw(near, q, 0)
     net.arrive(far, raw_slot(x, q + 2))
     net.send(far, ("raw", 1, 7), raw_slot(x, q + 2), net.device(dz=-1))
-    passed = both(factors, x >= q + 2)
-    send_raw(passed, q + 2, 1)
     for a in range(3):
         for zs in range(2):
             send_rows(z == zs, zs, a)
-    for b in range(4):
-        send_cols(top, b)
+        cols_along_y(top, a)
+        cols_along_x(both(top, relays), a)
+    cols_along_y(top, 3)
+    cols_along_x(both(top, relays), 3)
+    passed = both(factors, x >= q + 2)
+    send_raw(passed, q + 2, 1)
 
     across = lax.broadcasted_iota(jnp.int32, (128, 128), 1)
     down = lax.broadcasted_iota(jnp.int32, (128, 128), 0)
@@ -246,6 +246,8 @@
     for k in range(LEAD_TILES):
         if k == 0:
             raw_arrive(0, 0)
+            for b in range(4):
+                cols_along_x(factors, b)
 
         @pl.when(factors)
         def _():
@@ -283,39 +285,22 @@
             for a in range(3):
                 send_rows(factors, 1, a)
 
-    for a in range(3):
-        for zs in range(2):
-            send_rows(both(relays, z != zs), zs, a)
-        send_cols(jnp.logical_not(top), a)
-    send_cols(jnp.logical_not(top), 3)
-    for dx in range(1, NX):
-        for b in range(4):
-            net.arrive(always, col_slot((x + dx) % NX, b))
-    for zs in range(2):
-        for a in range(3):
-            net.arrive(always, row_slot(1 - q + 2 * zs, a))
-    for k in range(LEAD_TILES):
-        for b in range(4):
-            right[k, :, 128 * b : 128 * b + 128] = cols[k, b] * mask[k, b * 24 + c].astype(f32)
-        for a in range(3):
-            left[k, 128 * a : 128 * a + 128, :] = rows[k, a] * mask[a * 32 + r, k].astype(f32)
-    own_copy.wait()
-    for a in range(3):
-        for b in range(4):
-            schur[128 * a : 128 * a + 128, 128 * b : 128 * b + 128] = own[a, b] * mask[
-                a * 32 + r, b * 24 + c
-            ].astype(f32)
-
     passing = both(relays, top)
-    for k in range(LEAD_TILES):
+    below = jnp.logical_not(top)
+
+    def pass_piece(k):
         slot = piece_slot(k, piece_of)
         net.arrive(relays, slot)
         for n, peer in enumerate(net.column()):
             net.send(passing, ("piece", k, 11 + n), slot, peer)
         for n, peer in enumerate(net.group()):
             net.send(relays, ("piece", k, n), slot, peer)
+
+    def take_pieces(k):
         for n in range(1, 8):
             net.arrive(relays, piece_slot(k, (piece_of + n) % 8))
+
+    def apply_column(k):
         inverse = factor[k, 0]
         zk = dot(inverse, right[k])
         yk = dot(left[k], inverse, NT)
@@ -325,6 +310,43 @@
             right[i] = right[i] - dot(lower, zk)
             left[i] = left[i] - dot(yk, lower, NT)
         schur[...] = schur[...] - dot(yk, zk)
+
+    for b in range(4):
+        if b < 3:
+            for zs in range(2):
+                send_rows(both(relays, z != zs), zs, b)
+        cols_along_y(below, b)
+        cols_along_x(below, b)
+    pass_piece(0)
+    own_copy.wait()
+    for a in range(3):
+        for b in range(4):
+            schur[128 * a : 128 * a + 128, 128 * b : 128 * b + 128] = own[a, b] * mask[
+                a * 32 + r, b * 24 + c
+            ].astype(f32)
+    for dx in range(1, NX):
+        for b in range(4):
+            net.arrive(always, col_slot((x + dx) % NX, b))
+    for k in range(LEAD_TILES):
+        for b in range(4):
+            right[k, :, 128 * b : 128 * b + 128] = cols[k, b] * mask[k, b * 24 + c].astype(f32)
+    pass_piece(1)
+    for zs in range(2):
+        for a in range(3):
+            net.arrive(always, row_slot(1 - q + 2 * zs, a))
+    for k in range(LEAD_TILES):
+        for a in range(3):
+            left[k, 128 * a : 128 * a + 128, :] = rows[k, a] * mask[a * 32 + r, k].astype(f32)
+    take_pieces(0)
+    apply_column(0)
+    pass_piece(2)
+    take_pieces(1)
+    apply_column(1)
+    pass_piece(3)
+    take_pieces(2)
+    apply_column(2)
+    take_pieces(3)
+    apply_column(3)
 
     edge = jnp.minimum(c, 3)
     for a in range(3):

time: 83 us -> 71.5 us (0.86)
  Pallas kernels: 81 us -> 69.5 us
    pallas_call x1, Pallas kernels: 81 us -> 69.5 us  [on_device(): pl.pallas_call(kernel, out_shape=jax.ShapeDtypeStruct(covariance.shape, j...]
where the time goes in v3:
time: 71.5 us; the launch traced here: 71.3 us
  Pallas kernels  69.5 us (97%)
  local copies, waits for them, and re-layouts  1.77 us (2%)
    pallas_call x1, Pallas kernels, on_device(): pl.pallas_call(kernel, out_shape=jax.ShapeDtypeStruct(covariance.shape, j...  69.5 us
    unnamed x1, local copies, waits for them, and re-layouts  1.77 us

profile of v3, /device:TPU:457, one launch (start us, length us, event | category | flops | bytes accessed | tf_op | source)
XLA Modules:
  0.0 71.3 jit_solution(7875770726759167823)
XLA Ops:
  0.0 69.5 %panels.1 = bf16[3,1,4,1,128,128]{5,4,3,2,1,0:T(8,128)(2,1)} custom-call(s32[96,96]{1,0:T(8,128)} %mask.1, f32[3,1,4,1,128,128]{5,4,3,2,1,0:T(8,128)} %cov.1), custom_call_target="tpu_custom_call" | custom-call | tf_op jit(solution)/shard_map/panels/pallas_call | solution.py:368
  69.5 1.8 %copy.4 = bf16[3,1,4,1,128,128]{5,4,3,2,1,0:T(8,128)(2,1)} copy(bf16[3,1,4,1,128,128]{5,4,3,2,1,0:T(8,128)(2,1)} %panels.1) | data formatting | bytes 786432

commit v4 on v3

--- a/solution.py
+++ b/solution.py
@@ -73,6 +73,18 @@
                 work[q2:, :] = work[q2:, :] - dot(turned[q2:, :], both)
 
 
+def split(value):
+    high = value.astype(jnp.bfloat16)
+    return high, (value - high.astype(f32)).astype(jnp.bfloat16)
+
+
+def split_dot(a, b, dims=NN):
+    def part(i, j):
+        return lax.dot_general(a[i], b[j], dims, preferred_element_type=f32)
+
+    return part(0, 0) + (part(0, 1) + part(1, 0))
+
+
 class Net:
     def __init__(self, recv, sent):
         self.recv, self.sent = recv, sent
@@ -151,7 +163,7 @@
 
 RAW_SEM, ROW_SEM, COL_SEM, PIECE_SEM = 0, 16, 28, 44
 RECV_SEMS = 76
-SEND_SEMS = 125
+SEND_SEMS = 128
 
 
 def kernel(
@@ -207,6 +219,9 @@
         rel = (z - zs + NZ) % NZ
         up = rel <= 5
         down = jnp.logical_or(rel == 0, rel >= 8)
+        if zs == 1:
+            down = both(down, rel != 11)
+            net.send(both(cond, rel == 0), ("row", zs, a, 3), slot, net.device(dz=-2))
         net.send(both(cond, up), ("row", zs, a, 0), slot, net.device(dz=1))
         net.send(both(cond, down), ("row", zs, a, 1), slot, net.device(dz=-1))
         net.send(cond, ("row", zs, a, 2), slot, net.device(dq=1))
@@ -243,6 +258,10 @@
     def raw_arrive(i, k):
         net.arrive(both(factors, both(jnp.logical_or(x != i, q != k % 2), True)), raw_slot(i, k))
 
+    def subtract(i, j, k):
+        old = raw[i, j] if k == 0 else trail[i, j]
+        trail[i, j] = old - dot(factor[k, i - k], factor[k, j - k], NT)
+
     for k in range(LEAD_TILES):
         if k == 0:
             raw_arrive(0, 0)
@@ -253,6 +272,10 @@
         def _():
             work[:, 0:128] = raw[0, 0] if k == 0 else trail[k, k]
             work[:, 128:256] = (across == down).astype(f32)
+            for i in range(k + 1, LEAD_TILES):
+                for j in range(k, i + 1):
+                    if k > 0:
+                        subtract(i, j, k - 1)
             factor_tile(work)
             factor[k, 0] = work[:, 128:256]
 
@@ -274,12 +297,11 @@
                 for j in range(1, i + 1):
                     raw_arrive(i, j)
 
-        @pl.when(factors)
-        def _():
-            for i in range(k + 1, LEAD_TILES):
-                for j in range(k + 1, i + 1):
-                    old = raw[i, j] if k == 0 else trail[i, j]
-                    trail[i, j] = old - dot(factor[k, i - k], factor[k, j - k], NT)
+        if k < 3:
+
+            @pl.when(factors)
+            def _():
+                subtract(k + 1, k + 1, k)
 
         if k == 0:
             for a in range(3):
@@ -301,15 +323,16 @@
             net.arrive(relays, piece_slot(k, (piece_of + n) % 8))
 
     def apply_column(k):
-        inverse = factor[k, 0]
-        zk = dot(inverse, right[k])
-        yk = dot(left[k], inverse, NT)
+        inverse = split(factor[k, 0])
+        zk = split(split_dot(inverse, split(right[k])))
+        yk = split_dot(split(left[k]), inverse, NT)
         left[k] = yk
+        yk = split(yk)
         for i in range(k + 1, LEAD_TILES):
-            lower = factor[k, i - k]
-            right[i] = right[i] - dot(lower, zk)
-            left[i] = left[i] - dot(yk, lower, NT)
-        schur[...] = schur[...] - dot(yk, zk)
+            lower = split(factor[k, i - k])
+            right[i] = right[i] - split_dot(lower, zk)
+            left[i] = left[i] - split_dot(yk, lower, NT)
+        schur[...] = schur[...] - split_dot(yk, zk)
 
     for b in range(4):
         if b < 3:

time: 71.5 us -> 68.6 us (0.959)
  the two profiles are of different devices: /device:TPU:457 before, /device:TPU:481 now
where the time goes in v4:
time: 68.6 us; the launch traced here: 68.4 us
  Pallas kernels  66.6 us (97%)
  local copies, waits for them, and re-layouts  1.77 us (3%)
    pallas_call x1, Pallas kernels, on_device(): pl.pallas_call(kernel, out_shape=jax.ShapeDtypeStruct(covariance.shape, j...  66.6 us
    unnamed x1, local copies, waits for them, and re-layouts  1.77 us

profile of v4, /device:TPU:481, one launch (start us, length us, event | category | flops | bytes accessed | tf_op | source)
XLA Modules:
  0.0 68.4 jit_solution(11746860993062141849)
XLA Ops:
  0.0 66.6 %panels.1 = bf16[3,1,4,1,128,128]{5,4,3,2,1,0:T(8,128)(2,1)} custom-call(s32[96,96]{1,0:T(8,128)} %mask.1, f32[3,1,4,1,128,128]{5,4,3,2,1,0:T(8,128)} %cov.1), custom_call_target="tpu_custom_call" | custom-call | tf_op jit(solution)/shard_map/panels/pallas_call | solution.py:391
  66.6 1.8 %copy.4 = bf16[3,1,4,1,128,128]{5,4,3,2,1,0:T(8,128)(2,1)} copy(bf16[3,1,4,1,128,128]{5,4,3,2,1,0:T(8,128)(2,1)} %panels.1) | data formatting | bytes 786432

commit v5 on v4

--- a/solution.py
+++ b/solution.py
@@ -310,13 +310,13 @@
     passing = both(relays, top)
     below = jnp.logical_not(top)
 
-    def pass_piece(k):
+    def pass_piece(k, cond):
         slot = piece_slot(k, piece_of)
-        net.arrive(relays, slot)
+        net.arrive(cond, slot)
         for n, peer in enumerate(net.column()):
-            net.send(passing, ("piece", k, 11 + n), slot, peer)
+            net.send(both(cond, top), ("piece", k, 11 + n), slot, peer)
         for n, peer in enumerate(net.group()):
-            net.send(relays, ("piece", k, n), slot, peer)
+            net.send(cond, ("piece", k, n), slot, peer)
 
     def take_pieces(k):
         for n in range(1, 8):
@@ -334,13 +334,20 @@
             left[i] = left[i] - split_dot(yk, lower, NT)
         schur[...] = schur[...] - split_dot(yk, zk)
 
+    z_hops = jnp.where(z <= 6, z, NZ + 1 - z)
+    y_hops = jnp.minimum(y, NY - y)
+
+    def relay_rows(cond):
+        for a in range(3):
+            for zs in range(2):
+                send_rows(both(both(relays, z != zs), cond), zs, a)
+
+    relay_rows(z_hops <= y_hops)
     for b in range(4):
-        if b < 3:
-            for zs in range(2):
-                send_rows(both(relays, z != zs), zs, b)
         cols_along_y(below, b)
         cols_along_x(below, b)
-    pass_piece(0)
+    relay_rows(z_hops > y_hops)
+    pass_piece(0, relays)
     own_copy.wait()
     for a in range(3):
         for b in range(4):
@@ -353,19 +360,21 @@
     for k in range(LEAD_TILES):
         for b in range(4):
             right[k, :, 128 * b : 128 * b + 128] = cols[k, b] * mask[k, b * 24 + c].astype(f32)
-    pass_piece(1)
+    pass_piece(1, relays)
     for zs in range(2):
         for a in range(3):
             net.arrive(always, row_slot(1 - q + 2 * zs, a))
     for k in range(LEAD_TILES):
         for a in range(3):
             left[k, 128 * a : 128 * a + 128, :] = rows[k, a] * mask[a * 32 + r, k].astype(f32)
+    pass_piece(2, passing)
+    pass_piece(3, passing)
     take_pieces(0)
     apply_column(0)
-    pass_piece(2)
+    pass_piece(2, below)
     take_pieces(1)
     apply_column(1)
-    pass_piece(3)
+    pass_piece(3, below)
     take_pieces(2)
     apply_column(2)
     take_pieces(3)

time: 68.6 us -> 65.7 us (0.958)
  the two profiles are of different devices: /device:TPU:481 before, /device:TPU:33 now
where the time goes in v5:
time: 65.7 us; the launch traced here: 65.4 us
  Pallas kernels  63.6 us (97%)
  local copies, waits for them, and re-layouts  1.77 us (3%)
    pallas_call x1, Pallas kernels, on_device(): pl.pallas_call(kernel, out_shape=jax.ShapeDtypeStruct(covariance.shape, j...  63.6 us
    unnamed x1, local copies, waits for them, and re-layouts  1.77 us

profile of v5, /device:TPU:33, one launch (start us, length us, event | category | flops | bytes accessed | tf_op | source)
XLA Modules:
  0.0 65.4 jit_solution(11164646647156052712)
XLA Ops:
  0.0 63.6 %panels.1 = bf16[3,1,4,1,128,128]{5,4,3,2,1,0:T(8,128)(2,1)} custom-call(s32[96,96]{1,0:T(8,128)} %mask.1, f32[3,1,4,1,128,128]{5,4,3,2,1,0:T(8,128)} %cov.1), custom_call_target="tpu_custom_call" | custom-call | tf_op jit(solution)/shard_map/panels/pallas_call | solution.py:400
  63.6 1.8 %copy.4 = bf16[3,1,4,1,128,128]{5,4,3,2,1,0:T(8,128)(2,1)} copy(bf16[3,1,4,1,128,128]{5,4,3,2,1,0:T(8,128)(2,1)} %panels.1) | data formatting | bytes 786432

commit v6 on v5

--- a/solution.py
+++ b/solution.py
@@ -121,7 +121,7 @@
             pl.semaphore_signal(sem, inc=1, device_id=peer, device_id_type=MESH)
         pl.semaphore_wait(sem, len(peers))
 
-    def send(self, cond, key, slot, device):
+    def send(self, cond, key, slot, device, later=False):
         ref, sem = slot
         index = self.slots.setdefault(key, len(self.slots))
         copy = pltpu.make_async_remote_copy(
@@ -133,11 +133,14 @@
             device_id_type=MESH,
         )
 
-        @pl.when(cond)
-        def _():
-            copy.start()
+        if not later:
+
+            @pl.when(cond)
+            def _():
+                copy.start()
 
         self.started.append((cond, copy))
+        return copy
 
     def load(self, cond, source, slot):
         ref, sem = slot
@@ -234,10 +237,12 @@
         net.send(both(cond, up), ("col", b, 0), slot, net.device(dy=1))
         net.send(both(cond, down), ("col", b, 1), slot, net.device(dy=-1))
 
-    def cols_along_x(cond, b):
+    def cols_along_x(cond, b, later=False):
         slot = col_slot(x, b)
-        for dx in range(1, NX):
-            net.send(cond, ("col", b, 1 + dx), slot, net.device(dx=dx))
+        return [
+            net.send(cond, ("col", b, 1 + dx), slot, net.device(dx=dx), later)
+            for dx in range(1, NX)
+        ]
 
     send_raw(near, q, 0)
     net.arrive(far, raw_slot(x, q + 2))
@@ -258,6 +263,13 @@
     def raw_arrive(i, k):
         net.arrive(both(factors, both(jnp.logical_or(x != i, q != k % 2), True)), raw_slot(i, k))
 
+    def piece_copies(k):
+        slot = piece_slot(k, piece_of)
+        return [
+            net.send(factors, ("piece", k, n), slot, peer, later=True)
+            for n, peer in enumerate(net.column() + net.ring())
+        ]
+
     def subtract(i, j, k):
         old = raw[i, j] if k == 0 else trail[i, j]
         trail[i, j] = old - dot(factor[k, i - k], factor[k, j - k], NT)
@@ -265,8 +277,9 @@
     for k in range(LEAD_TILES):
         if k == 0:
             raw_arrive(0, 0)
-            for b in range(4):
-                cols_along_x(factors, b)
+            held = [copy for b in range(4) for copy in cols_along_x(factors, b, later=True)]
+        else:
+            held = piece_copies(k - 1)
 
         @pl.when(factors)
         def _():
@@ -276,6 +289,8 @@
                 for j in range(k, i + 1):
                     if k > 0:
                         subtract(i, j, k - 1)
+            for copy in held:
+                copy.start()
             factor_tile(work)
             factor[k, 0] = work[:, 128:256]
 
@@ -289,9 +304,15 @@
                 tile = raw[i, 0] if k == 0 else trail[i, k]
                 factor[k, i - k] = dot(tile, work[:, 128:256], NT)
 
-        slot = piece_slot(k, piece_of)
-        for n, peer in enumerate(net.ring() + net.column()):
-            net.send(factors, ("piece", k, n), slot, peer)
+        if k == 3:
+
+            held = piece_copies(3)
+
+            @pl.when(factors)
+            def _():
+                for copy in held:
+                    copy.start()
+
         if k == 0:
             for i in range(1, LEAD_TILES):
                 for j in range(1, i + 1):
@@ -303,9 +324,8 @@
             def _():
                 subtract(k + 1, k + 1, k)
 
-        if k == 0:
-            for a in range(3):
-                send_rows(factors, 1, a)
+    for a in range(3):
+        send_rows(factors, 1, a)
 
     passing = both(relays, top)
     below = jnp.logical_not(top)

time: 65.7 us -> 63.8 us (0.971)
  Pallas kernels: 63.6 us -> 61.7 us
    pallas_call x1, Pallas kernels: 63.6 us -> 61.7 us  [on_device(): pl.pallas_call(kernel, out_shape=jax.ShapeDtypeStruct(covariance.shape, j...]
where the time goes in v6:
time: 63.8 us; the launch traced here: 63.5 us
  Pallas kernels  61.7 us (97%)
  local copies, waits for them, and re-layouts  1.77 us (3%)
    pallas_call x1, Pallas kernels, on_device(): pl.pallas_call(kernel, out_shape=jax.ShapeDtypeStruct(covariance.shape, j...  61.7 us
    unnamed x1, local copies, waits for them, and re-layouts  1.77 us

profile of v6, /device:TPU:33, one launch (start us, length us, event | category | flops | bytes accessed | tf_op | source)
XLA Modules:
  0.0 63.5 jit_solution(11432657243661878689)
XLA Ops:
  0.0 61.7 %panels.1 = bf16[3,1,4,1,128,128]{5,4,3,2,1,0:T(8,128)(2,1)} custom-call(s32[96,96]{1,0:T(8,128)} %mask.1, f32[3,1,4,1,128,128]{5,4,3,2,1,0:T(8,128)} %cov.1), custom_call_target="tpu_custom_call" | custom-call | tf_op jit(solution)/shard_map/panels/pallas_call | solution.py:420
  61.7 1.8 %copy.4 = bf16[3,1,4,1,128,128]{5,4,3,2,1,0:T(8,128)(2,1)} copy(bf16[3,1,4,1,128,128]{5,4,3,2,1,0:T(8,128)(2,1)} %panels.1) | data formatting | bytes 786432
